TPU v7x, 32 devices: a whole 2x2x4 slice. The times are simulated.
32 devices in a mesh: grp: 4 (over y, core), rep: 8 (over z, x).
Axes of the slice: x: 2, y: 2, z: 4, core: 2. Of those that a mesh axis runs over, the one named last changes fastest.
Arguments:
- tokens: bfloat16 [32, 1024, 768], P(('grp', 'rep')), may hold values from -6 to 6
- segment_ids: int32 [32, 1024], P(('grp', 'rep')), may hold values from 0 to 2, as said below
- cotangent: bfloat16 [32, 1024, 768], P(('grp', 'rep')), may hold values from -6 to 6
- in_proj_master: float32 [768, 3352], P('grp'), may hold values from -0.21875 to 0.21875
- out_proj_master: float32 [1536, 768], P('grp'), may hold values from -0.15625 to 0.15625
- in_proj_error: float32 [8, 768, 3352], P('rep', 'grp'), may hold values from -6 to 6
- out_proj_error: float32 [8, 1536, 768], P('rep', 'grp'), may hold values from -6 to 6
- in_proj_moment: float32 [768, 3352], P('grp'), may hold values from -6 to 6
- out_proj_moment: float32 [1536, 768], P('grp'), may hold values from -6 to 6
- in_proj_start: float32 [4, 3352, 8], P('grp'), may hold values from -6 to 6
- out_proj_start: float32 [4, 768, 8], P('grp'), may hold values from -6 to 6
- conv_master: float32 [5, 1792], replicated, may hold values from -3 to 3
- conv_moment: float32 [5, 1792], replicated, may hold values from -6 to 6
- head_master: float32 [3, 24], replicated, may hold values from -8 to 2, as said below
- head_moment: float32 [3, 24], replicated, may hold values from -6 to 6
- norm_gain: float32 [768], replicated, may hold values from 0.5 to 1.5
- norm_gain_moment: float32 [768], replicated, may hold values from -6 to 6
- gate_gain: float32 [1536], replicated, may hold values from 0.5 to 1.5
- gate_gain_moment: float32 [1536], replicated, may hold values from -6 to 6
Outputs:
- output: bfloat16 [32, 1024, 768], P(('grp', 'rep'))
- input_grad: float32 [32, 1024, 768], P(('grp', 'rep'))
- in_proj_grad: float32 [8, 768, 3352], P('rep', 'grp')
- out_proj_grad: float32 [8, 1536, 768], P('rep', 'grp')
- in_proj_left: float32 [768, 8], P('grp')
- out_proj_left: float32 [1536, 8], P('grp')
- in_proj_right: float32 [4, 3352, 8], P('grp')
- out_proj_right: float32 [4, 768, 8], P('grp')
- in_proj_error_new: float32 [8, 768, 3352], P('rep', 'grp')
- out_proj_error_new: float32 [8, 1536, 768], P('rep', 'grp')
- in_proj_moment_new: float32 [768, 3352], P('grp')
- out_proj_moment_new: float32 [1536, 768], P('grp')
- in_proj_master_new: float32 [768, 3352], P('grp')
- out_proj_master_new: float32 [1536, 768], P('grp')
- conv_grad: float32 [5, 1792], replicated
- conv_moment_new: float32 [5, 1792], replicated
- conv_master_new: float32 [5, 1792], replicated
- head_grad: float32 [3, 24], replicated
- head_moment_new: float32 [3, 24], replicated
- head_master_new: float32 [3, 24], replicated
- norm_gain_grad: float32 [768], replicated
- norm_gain_moment_new: float32 [768], replicated
- norm_gain_new: float32 [768], replicated
- gate_gain_grad: float32 [1536], replicated
- gate_gain_moment_new: float32 [1536], replicated
- gate_gain_new: float32 [1536], replicated
Inputs may be any that keep to these rules, and one draw needn't show every extreme that they name: `segment_ids`: within each sequence the ids never fall and all 3 ids occur; each document has 204 to 512 tokens and one has exactly 512. `head_master`: row 0 is the step bias, row 1 the log of the decay rate, row 2 the skip gain.
All inputs are finite; a program needn't handle non-finite values.
Results may differ from a plain program's by a relative error of at most 0.011.
Values may be sent and summed in bfloat16 or wider, within the bound.
No kernel may reach another device: no remote copies, remote signals or barrier semaphores. Data moves between devices by JAX's collectives and lax.ppermute only.
A program may use at most 256 MiB of HBM per device.

v0:
```python
import jax
import jax.numpy as jnp
from jax import lax
from jax.sharding import PartitionSpec as P

HEADS = 24
HEADDIM = 64
STATE = 128
CONV = 4
SPAN = 256
INNER = 1536
CONVDIM = 1792
EPS = 1e-05
GS_EPS = 1e-06
MOMENTUM = 0.9
RATE = 0.01
HIGH = lax.Precision.HIGHEST


def prenorm(inputs, gain):
    return inputs * lax.rsqrt(jnp.mean(inputs * inputs, axis=-1, keepdims=True) + EPS) * gain


def conv_part(projected, conv_params, head_params, segments):
    gate_in = projected[:, :INNER]
    conv_in = projected[:, INNER : INNER + CONVDIM]
    raw_steps = projected[:, INNER + CONVDIM :]
    summed = jnp.broadcast_to(conv_params[CONV], conv_in.shape)
    for offset in range(CONV):
        tap_row = conv_params[CONV - 1 - offset]
        if offset == 0:
            summed = summed + tap_row * conv_in
        else:
            shifted = jnp.pad(conv_in[:-offset], ((offset, 0), (0, 0)))
            earlier = jnp.pad(segments[:-offset], (offset, 0), constant_values=-1)
            same_doc = (earlier == segments).astype(jnp.float32)
            summed = summed + tap_row * shifted * same_doc[:, None]
    active = jax.nn.silu(summed)
    step_sizes = jax.nn.softplus(raw_steps + head_params[0])
    return (gate_in, active, step_sizes)


def span_step(carry, block):
    state, last_doc = carry
    values, sizes, decay_log, in_b, out_c, docs = block
    positions = docs.shape[0]
    heads_vals = values.reshape(positions, HEADS, HEADDIM)
    cumul = jnp.cumsum(decay_log, axis=1)
    places = jnp.arange(positions)
    allowed = (places[:, None] >= places[None, :]) & (docs[:, None] == docs[None, :])
    spread = cumul[:, :, None] - cumul[:, None, :]
    mask_three = allowed[None, :, :]
    decays = jnp.where(mask_three, jnp.exp(jnp.where(mask_three, spread, 0.0)), 0.0)
    inner_prod = jnp.dot(out_c, in_b.T, precision=HIGH)
    mixing = inner_prod[None, :, :] * decays * sizes[:, None, :]
    local_out = jnp.einsum("hij,jhp->ihp", mixing, heads_vals, precision=HIGH)
    alive = (docs == last_doc).astype(jnp.float32)
    carried = jnp.einsum("in,hpn->ihp", out_c, state, precision=HIGH)
    carried = carried * (jnp.exp(cumul).T * alive[:, None])[:, :, None]
    tail_weight = (
        jnp.exp(cumul[:, -1:] - cumul) * (docs == docs[-1]).astype(jnp.float32)[None, :] * sizes
    )
    keep_rate = jnp.exp(cumul[:, -1]) * (docs[-1] == last_doc).astype(jnp.float32)
    added = jnp.einsum("jhp,jn->hpn", tail_weight.T[:, :, None] * heads_vals, in_b, precision=HIGH)
    new_state = state * keep_rate[:, None, None] + added
    return ((new_state, docs[-1]), (local_out + carried).reshape(positions, INNER))


def spanned_scan(values, sizes, decay_log, in_b, out_c, segments):
    length = values.shape[0]
    blocks = length // SPAN
    pieces = (
        values.reshape(blocks, SPAN, INNER),
        jnp.swapaxes(sizes.reshape(blocks, SPAN, HEADS), 1, 2),
        jnp.swapaxes(decay_log.reshape(blocks, SPAN, HEADS), 1, 2),
        in_b.reshape(blocks, SPAN, STATE),
        out_c.reshape(blocks, SPAN, STATE),
        segments.reshape(blocks, SPAN),
    )
    start = (jnp.zeros((HEADS, HEADDIM, STATE), jnp.float32), jnp.array(-1, jnp.int32))
    ended, outputs = lax.scan(jax.checkpoint(span_step), start, pieces)
    return outputs.reshape(length, INNER)


def mixer_part(active, step_sizes, gate_in, head_params, gate_gain, segments):
    values = active[:, :INNER]
    in_b = active[:, INNER : INNER + STATE]
    out_c = active[:, INNER + STATE :]
    decay_log = -step_sizes * jnp.exp(head_params[1])
    scanned = spanned_scan(values, step_sizes, decay_log, in_b, out_c, segments)
    skip_row = jnp.repeat(head_params[2], HEADDIM)
    result = scanned + skip_row[None, :] * values
    gated = result * jax.nn.silu(gate_in)
    return gated * lax.rsqrt(jnp.mean(gated * gated, axis=-1, keepdims=True) + EPS) * gate_gain


def orthogonal(matrix):
    columns = []
    for index in range(matrix.shape[1]):
        vector = matrix[:, index]
        for done in columns:
            vector = vector - jnp.sum(done * vector) * done
        vector = vector * lax.rsqrt(jnp.sum(vector * vector) + GS_EPS)
        columns.append(vector)
    return jnp.stack(columns, axis=1)


def contract_rows(left_mat, right_mat, precision_kind):
    return lax.dot_general(
        left_mat,
        right_mat,
        (((0,), (0,)), ((), ())),
        precision=precision_kind,
        preferred_element_type=jnp.float32,
    )


def plain_update(grad_sum, moment, master, replicas):
    moment_new = MOMENTUM * moment + grad_sum / replicas
    return (moment_new, master - RATE * moment_new)


def on_device(
    tokens,
    segment_ids,
    cotangent,
    in_proj_master,
    out_proj_master,
    in_proj_error,
    out_proj_error,
    in_proj_moment,
    out_proj_moment,
    in_proj_start,
    out_proj_start,
    conv_master,
    conv_moment,
    head_master,
    head_moment,
    norm_gain,
    norm_gain_moment,
    gate_gain,
    gate_gain_moment,
):
    replicas = lax.axis_size("rep")
    w_in, w_out = (
        lax.all_gather(in_proj_master.astype(jnp.bfloat16), "grp", axis=0, tiled=True),
        lax.all_gather(out_proj_master.astype(jnp.bfloat16), "grp", axis=0, tiled=True),
    )
    seq_count, seq_len, width = tokens.shape
    row_count = seq_count * seq_len
    inputs = tokens.astype(jnp.float32)
    normed, norm_back = jax.vjp(prenorm, inputs, norm_gain)
    normed_low = normed.astype(jnp.bfloat16).reshape(row_count, width)
    projected = jnp.dot(normed_low, w_in, preferred_element_type=jnp.float32).reshape(
        seq_count, seq_len, -1
    )

    def first_part(proj_all, conv_params, head_params):
        return jax.vmap(conv_part, in_axes=(0, None, None, 0))(
            proj_all, conv_params, head_params, segment_ids
        )

    (gate_in, active, step_sizes), first_back = jax.vjp(
        first_part, projected, conv_master, head_master
    )
    active_low = lax.optimization_barrier(active.astype(jnp.bfloat16)).astype(jnp.float32)

    def second_part(active_all, sizes_all, gates_all, head_params, out_gain):
        return jax.vmap(mixer_part, in_axes=(0, 0, 0, None, None, 0))(
            active_all, sizes_all, gates_all, head_params, out_gain, segment_ids
        )

    mixed, second_back = jax.vjp(
        second_part, active_low, step_sizes, gate_in, head_master, gate_gain
    )
    mixed_low = mixed.astype(jnp.bfloat16).reshape(row_count, INNER)
    branch = jnp.dot(mixed_low, w_out, preferred_element_type=jnp.float32)
    output = (inputs + branch.reshape(tokens.shape)).astype(jnp.bfloat16)
    cot_rows = cotangent.reshape(row_count, width)
    d_mixed = lax.dot_general(
        cot_rows, w_out, (((1,), (1,)), ((), ())), preferred_element_type=jnp.float32
    )
    out_local = contract_rows(mixed_low, cot_rows, None)
    d_active, d_sizes, d_gates, d_heads_two, d_gate_gain = second_back(d_mixed.reshape(mixed.shape))
    d_projected, d_conv, d_heads_one = first_back((d_gates, d_active, d_sizes))
    d_proj_low = d_projected.astype(jnp.bfloat16).reshape(row_count, -1)
    in_local = contract_rows(normed_low, d_proj_low, None)
    d_normed = lax.dot_general(
        d_proj_low, w_in, (((1,), (1,)), ((), ())), preferred_element_type=jnp.float32
    )
    d_inputs, d_norm_gain = norm_back(d_normed.reshape(normed.shape))
    input_grad = cotangent.astype(jnp.float32) + d_inputs
    in_shard, out_shard = (
        lax.psum_scatter(in_local, "grp", scatter_dimension=0, tiled=True),
        lax.psum_scatter(out_local, "grp", scatter_dimension=0, tiled=True),
    )
    d_heads = d_heads_one + d_heads_two
    whole_in = in_shard + in_proj_error[0]
    whole_out = out_shard + out_proj_error[0]
    left_in = jnp.dot(whole_in, in_proj_start[0], precision=HIGH)
    left_out = jnp.dot(whole_out, out_proj_start[0], precision=HIGH)
    conv_grad, head_grad, norm_gain_grad, gate_gain_grad = lax.psum(
        (d_conv, d_heads, d_norm_gain, d_gate_gain), ("grp", "rep")
    )
    left_in, left_out = lax.psum((left_in, left_out), "rep")
    hat_in = orthogonal(left_in)
    hat_out = orthogonal(left_out)
    right_in = contract_rows(whole_in, hat_in, HIGH)
    right_out = contract_rows(whole_out, hat_out, HIGH)
    right_in, right_out = lax.psum((right_in, right_out), "rep")
    right_in = right_in / replicas
    right_out = right_out / replicas
    approx_in = jnp.dot(hat_in, right_in.T, precision=HIGH)
    approx_out = jnp.dot(hat_out, right_out.T, precision=HIGH)
    in_mom = MOMENTUM * in_proj_moment + approx_in
    out_mom = MOMENTUM * out_proj_moment + approx_out
    in_new = in_proj_master - RATE * in_mom
    out_new = out_proj_master - RATE * out_mom
    conv_mom, conv_new = plain_update(conv_grad, conv_moment, conv_master, replicas)
    head_mom, head_new = plain_update(head_grad, head_moment, head_master, replicas)
    gain_mom, gain_new = plain_update(norm_gain_grad, norm_gain_moment, norm_gain, replicas)
    gate_mom, gate_new = plain_update(gate_gain_grad, gate_gain_moment, gate_gain, replicas)
    return (
        output,
        input_grad,
        in_shard[None],
        out_shard[None],
        hat_in,
        hat_out,
        right_in[None],
        right_out[None],
        (whole_in - approx_in)[None],
        (whole_out - approx_out)[None],
        in_mom,
        out_mom,
        in_new,
        out_new,
        conv_grad,
        conv_mom,
        conv_new,
        head_grad,
        head_mom,
        head_new,
        norm_gain_grad,
        gain_mom,
        gain_new,
        gate_gain_grad,
        gate_mom,
        gate_new,
    )


def solution(mesh):
    return jax.shard_map(
        on_device,
        mesh=mesh,
        in_specs=(
            P(("grp", "rep"), None, None),
            P(("grp", "rep"), None),
            P(("grp", "rep"), None, None),
            P("grp", None),
            P("grp", None),
            P("rep", "grp", None),
            P("rep", "grp", None),
            P("grp", None),
            P("grp", None),
            P("grp", None, None),
            P("grp", None, None),
            P(),
            P(),
            P(),
            P(),
            P(),
            P(),
            P(),
            P(),
        ),
        out_specs=(
            P(("grp", "rep"), None, None),
            P(("grp", "rep"), None, None),
            P("rep", "grp", None),
            P("rep", "grp", None),
            P("grp", None),
            P("grp", None),
            P("grp", None, None),
            P("grp", None, None),
            P("rep", "grp", None),
            P("rep", "grp", None),
            P("grp", None),
            P("grp", None),
            P("grp", None),
            P("grp", None),
            P(),
            P(),
            P(),
            P(),
            P(),
            P(),
            P(),
            P(),
            P(),
            P(),
            P(),
            P(),
        ),
        check_vma=False,
    )
```

profile of v0, /device:TPU:0, one launch (start us, length us, event | category | flops | bytes accessed | tf_op | source)
XLA Modules:
  0.0 1407.3 jit_solution(13596165531728517373)
XLA Ops:
  14.2 39.9 %all-gather.3.cloned.1.call-done = bf16[768,3352]{1,0:T(8,128)(2,1)} async-done(((bf16[192,3352]{1,0:T(8,128)(2,1)}), bf16[768,3352]{1,0:T(8,128)(2,1)}) %all-gather.3.cloned.1.call-update) | async-done | bytes 5148688 | tf_op jit(solution)/shard_map/all_gather | solution.py:146
  75.4 15.0 %multiply_convert_fusion = (bf16[1,1024,1792]{1,2,0:T(8,128)(2,1)S(1)}, f32[1,1024,1792]{1,2,0:T(8,128)}) fusion(f32[1024]{0:T(1024)S(1)} %bitcast.693, f32[1,1021,1792]{1,2,0:T(8,128)} %slice.251, f32[1792]{0:T(1024)S(1)} %get-tuple-element.791, f32[1024]{0:T(1024)S(1)} %bitcast.691, f32[1,1022,1792]{1,2,0:T(8,128)} %slice.250, ...), kind=kLoop, calls=%fused_computation.159 | loop fusion | flops 29360128 | bytes 40375296 | tf_op jit(solution)/shard_map/convert_element_type | solution.py:166
  108.7 254.1 %while.46 = (s32[]{:T(128)}, f32[1,24,64,128]{3,2,1,0:T(8,128)S(1)}, s32[1]{0:T(128)}, f32[4,1,256,1536]{2,0,3,1:T(4,128)}, f32[4,1,24,64,128]{4,3,2,1,0:T(8,128...) while((s32[]{:T(128)}, ...), condition=%wide.region_4.5_spmd.clone, body=%wide.region_1.4_spmd.clone.sunk | while | flops 2527624192 | bytes 27957864 | solution.py:81
  137.4 34.2 %dynamic_update_slice.88 = f32[4,1,256,1536]{2,0,3,1:T(4,128)} dynamic-update-slice(f32[4,1,256,1536]{2,0,3,1:T(4,128)} %get-tuple-element.1300, f32[1,1,256,1536]{2,0,3,1:T(1,128)S(1)} %copy.412, s32[]{:T(128)S(6)} %copy.447, s32[]{:T(128)} %constant.161.clone.1..sunk, s32[]{:T(128)} %constant.161.clone.1..sunk, s32[]{:T(128)} %constant.161.clone.1..sunk) | dynamic-update-slice | bytes 3145732 | tf_op jit(solution)/shard_map/jvp(vmap())/while/body/jit(dynamic_update_index_in_dim)/dynamic_update_slice | solution.py:81
  200.9 34.2 %dynamic_update_slice.88 = f32[4,1,256,1536]{2,0,3,1:T(4,128)} dynamic-update-slice(f32[4,1,256,1536]{2,0,3,1:T(4,128)} %get-tuple-element.1300, f32[1,1,256,1536]{2,0,3,1:T(1,128)S(1)} %copy.412, s32[]{:T(128)S(6)} %copy.447, s32[]{:T(128)} %constant.161.clone.1..sunk, s32[]{:T(128)} %constant.161.clone.1..sunk, s32[]{:T(128)} %constant.161.clone.1..sunk) | dynamic-update-slice | bytes 3145732 | tf_op jit(solution)/shard_map/jvp(vmap())/while/body/jit(dynamic_update_index_in_dim)/dynamic_update_slice | solution.py:81
  264.5 34.2 %dynamic_update_slice.88 = f32[4,1,256,1536]{2,0,3,1:T(4,128)} dynamic-update-slice(f32[4,1,256,1536]{2,0,3,1:T(4,128)} %get-tuple-element.1300, f32[1,1,256,1536]{2,0,3,1:T(1,128)S(1)} %copy.412, s32[]{:T(128)S(6)} %copy.447, s32[]{:T(128)} %constant.161.clone.1..sunk, s32[]{:T(128)} %constant.161.clone.1..sunk, s32[]{:T(128)} %constant.161.clone.1..sunk) | dynamic-update-slice | bytes 3145732 | tf_op jit(solution)/shard_map/jvp(vmap())/while/body/jit(dynamic_update_index_in_dim)/dynamic_update_slice | solution.py:81
  328.0 34.2 %dynamic_update_slice.88 = f32[4,1,256,1536]{2,0,3,1:T(4,128)} dynamic-update-slice(f32[4,1,256,1536]{2,0,3,1:T(4,128)} %get-tuple-element.1300, f32[1,1,256,1536]{2,0,3,1:T(1,128)S(1)} %copy.412, s32[]{:T(128)S(6)} %copy.447, s32[]{:T(128)} %constant.161.clone.1..sunk, s32[]{:T(128)} %constant.161.clone.1..sunk, s32[]{:T(128)} %constant.161.clone.1..sunk) | dynamic-update-slice | bytes 3145732 | tf_op jit(solution)/shard_map/jvp(vmap())/while/body/jit(dynamic_update_index_in_dim)/dynamic_update_slice | solution.py:81
  401.2 19.5 %multiply_reduce_fusion.8 = (f32[1536]{0:T(1024)}, f32[1,1024,1536]{1,2,0:T(8,128)}, f32[1,1024,1536]{1,2,0:T(8,128)}) fusion(f32[1,1024,1792]{1,2,0:T(8,128)} %convert_element_type.87, f32[1,1024,3352]{1,2,0:T(8,128)} %copy-done.1, f32[1,1024,1536]{1,2,0:T(8,128)} %copy-done.7, f32[1024]{0:T(1024)S(1)} %multiply_multiply_fusion.1, f32[1024]{0:T(1024)S(1)} %fusion.124, ...), kind=kLoop, calls=%fused_computation.170 | loop fusion | flops 33028608 | bytes 44066816 | tf_op jit(solution)/shard_map/transpose(jvp(vmap()))/reduce_sum | solution.py:92
  435.3 512.2 %while.47 = (s32[]{:T(128)}, f32[1,24,64,128]{3,2,1,0:T(8,128)S(1)}, f32[4,1,256,1536]{2,0,3,1:T(4,128)}, f32[4,1,24,256]{2,3,1,0:T(8,128)}, f32[4,1,24,256]{3,0...) while((s32[]{:T(128)}, ...), condition=%wide.region_20.21_spmd.clone, body=%wide.region_7.20_spmd.clone.sunk | while | flops 5775293440 | bytes 58667620 | solution.py:81
  529.3 34.1 %dynamic_update_slice.92 = f32[4,1,256,1536]{2,0,3,1:T(4,128)} dynamic-update-slice(f32[4,1,256,1536]{2,0,3,1:T(4,128)} %get-tuple-element.1349, f32[1,1,256,1536]{2,0,3,1:T(1,128)S(1)} %copy.427, s32[]{:T(128)S(6)} %sub.1200, s32[]{:T(128)} %constant.161.clone.1..sunk.1, s32[]{:T(128)} %constant.161.clone.1..sunk.1, s32[]{:T(128)} %constant.161.clone.1..sunk.1) | dynamic-update-slice | bytes 3145732 | tf_op jit(solution)/shard_map/transpose(jvp(vmap()))/while/body/jit(dynamic_update_index_in_dim)/dynamic_update_slice | solution.py:81
  598.9 12.0 fusion.249
  657.3 34.1 %dynamic_update_slice.92 = f32[4,1,256,1536]{2,0,3,1:T(4,128)} dynamic-update-slice(f32[4,1,256,1536]{2,0,3,1:T(4,128)} %get-tuple-element.1349, f32[1,1,256,1536]{2,0,3,1:T(1,128)S(1)} %copy.427, s32[]{:T(128)S(6)} %sub.1200, s32[]{:T(128)} %constant.161.clone.1..sunk.1, s32[]{:T(128)} %constant.161.clone.1..sunk.1, s32[]{:T(128)} %constant.161.clone.1..sunk.1) | dynamic-update-slice | bytes 3145732 | tf_op jit(solution)/shard_map/transpose(jvp(vmap()))/while/body/jit(dynamic_update_index_in_dim)/dynamic_update_slice | solution.py:81
  785.2 34.1 %dynamic_update_slice.92 = f32[4,1,256,1536]{2,0,3,1:T(4,128)} dynamic-update-slice(f32[4,1,256,1536]{2,0,3,1:T(4,128)} %get-tuple-element.1349, f32[1,1,256,1536]{2,0,3,1:T(1,128)S(1)} %copy.427, s32[]{:T(128)S(6)} %sub.1200, s32[]{:T(128)} %constant.161.clone.1..sunk.1, s32[]{:T(128)} %constant.161.clone.1..sunk.1, s32[]{:T(128)} %constant.161.clone.1..sunk.1) | dynamic-update-slice | bytes 3145732 | tf_op jit(solution)/shard_map/transpose(jvp(vmap()))/while/body/jit(dynamic_update_index_in_dim)/dynamic_update_slice | solution.py:81
  913.1 34.1 %dynamic_update_slice.92 = f32[4,1,256,1536]{2,0,3,1:T(4,128)} dynamic-update-slice(f32[4,1,256,1536]{2,0,3,1:T(4,128)} %get-tuple-element.1349, f32[1,1,256,1536]{2,0,3,1:T(1,128)S(1)} %copy.427, s32[]{:T(128)S(6)} %sub.1200, s32[]{:T(128)} %constant.161.clone.1..sunk.1, s32[]{:T(128)} %constant.161.clone.1..sunk.1, s32[]{:T(128)} %constant.161.clone.1..sunk.1) | dynamic-update-slice | bytes 3145732 | tf_op jit(solution)/shard_map/transpose(jvp(vmap()))/while/body/jit(dynamic_update_index_in_dim)/dynamic_update_slice | solution.py:81
  969.8 13.0 multiply_reduce_fusion.7
  1013.7 14.6 %multiply_reduce_fusion.4 = (f32[1792]{0:T(1024)S(1)}, f32[1792]{0:T(1024)S(1)}, f32[1,1024,1792]{1,2,0:T(8,128)}) fusion(f32[1,1024,1792]{1,2,0:T(8,128)S(1)} %bitcast.641, f32[1,1024,3352]{1,2,0:T(8,128)} %copy-done.1, f32[1792]{0:T(1024)S(1)} %copy-done.34, f32[1,1023,1792]{1,2,0:T(8,128)} %slice_multiply_fusion, ...), kind=kLoop, calls=%fused_computation.154 | loop fusion | flops 12841472 | bytes 44018688 | tf_op jit(solution)/shard_map/transpose(jvp(vmap()))/reduce_sum | solution.py:32
  1028.4 15.2 %fusion.107 = f32[768,3352]{1,0:T(8,128)} fusion(bf16[1,1024,768]{2,1,0:T(8,128)(2,1)S(1)} %copy-done.13, f32[768]{0:T(1024)S(1)} %copy-done.50, f32[1024]{0:T(1024)S(1)} %copy-done.52, f32[1,1024,1536]{1,2,0:T(8,128)} %get-tuple-element.1023, f32[1,1024,1792]{1,2,0:T(8,128)} %get-tuple-element.1024, f32[1,1024,24]{1,2,0:T(8,128)S(1)} %get-tuple-element.931), kind=kOutput, calls=%fused_computation.210 | convolution fusion | flops 5285683200 | bytes 25607168 | tf_op jit(solution)/shard_map/dot_general | solution.py:109
  1045.9 14.0 fusion.94
  1059.9 41.2 %all-reduce.25 = (f32[5,1792]{1,0:T(8,128)S(1)}, f32[3,24]{1,0:T(4,128)S(1)}, f32[768]{0:T(1024)S(1)}, f32[1536]{0:T(1024)S(1)}) all-reduce(f32[5,1792]{1,0:T(8,128)S(1)} %pad_add_fusion, f32[3,24]{1,0:T(4,128)} %add_add_fusion.2, f32[768]{0:T(1024)} %get-tuple-element.785, ...), channel_id=1, replica_groups=mesh['grp'=4,'rep'=8] {'grp','rep'}, use_global_device_ids=true, to_apply=%region_105.106 | all-reduce | flops 11336 | bytes 90688 | tf_op jit(solution)/shard_map/psum | solution.py:202
  1120.3 37.0 %psum.57 = f32[384,8]{0,1:T(8,128)S(1)} all-reduce(f32[384,8]{0,1:T(8,128)S(1)} %fusion.118), channel_id=1, replica_groups=mesh['grp'=4,'rep'=8] {'rep'}, use_global_device_ids=true, to_apply=%region_61.62 | all-reduce | flops 3072 | bytes 24576 | tf_op jit(solution)/shard_map/psum | solution.py:205
  1200.7 17.7 %subtract_multiply_fusion.2 = (f32[384,1]{0,1:T(1,128)S(1)}, f32[384,1]{0,1:T(1,128)S(1)}, f32[384,1]{0,1:T(1,128)S(1)}, f32[384,1]{0,1:T(1,128)S(1)}, f32[384,1...) fusion(f32[384,1]{0,1:T(1,128)S(1)} %get-tuple-element.1004, f32[384,8]{0,1:T(8,128)S(1)} %psum.57, ...), kind=kLoop, calls=%fused_computation.318 | loop fusion | flops 24192 | bytes 23180 | tf_op jit(solution)/shard_map/mul | solution.py:103
  1224.9 33.4 %all-reduce.26 = (f32[192,8]{0,1:T(8,128)S(1)}, f32[768,8]{0,1:T(8,128)S(1)}) all-reduce(f32[192,8]{0,1:T(8,128)S(1)} %fusion.110, f32[768,8]{0,1:T(8,128)S(1)} %fusion.128), channel_id=1, replica_groups=mesh['grp'=4,'rep'=8] {'rep'}, use_global_device_ids=true, to_apply=%region_24.25 | all-reduce | flops 7680 | bytes 61440 | tf_op jit(solution)/shard_map/psum | solution.py:205
  1300.2 17.6 %subtract_multiply_fusion.9 = (f32[192,1]{0,1:T(1,128)S(1)}, f32[192,1]{0,1:T(1,128)S(1)}, f32[192,1]{0,1:T(1,128)S(1)}, f32[192,1]{0,1:T(1,128)S(1)}, f32[192,1...) fusion(f32[192,1]{0,1:T(1,128)S(1)} %get-tuple-element.1033, f32[]{:T(128)S(6)} %rsqrt.79, ...), kind=kLoop, calls=%fused_computation.331 | loop fusion | flops 12096 | bytes 11660 | tf_op jit(solution)/shard_map/mul | solution.py:103
  1328.1 61.1 %all-reduce.29.cloned.1.call-done = f32[3352,8]{0,1:T(8,128)} async-done(((f32[3352,8]{0,1:T(8,128)}), f32[3352,8]{0,1:T(8,128)}) %all-reduce.29.cloned.1.call-update) | async-done | bytes 107280 | tf_op jit(solution)/shard_map/psum | solution.py:210
  (693 shorter events, 744.7 us)
Async XLA Ops:
  7.2 1213.6 %copy-start = (f32[1,3352,8]{1,2,0:T(8,128)S(1)}, f32[1,3352,8]{1,2,0:T(8,128)}, u32[]{:S(2)}) copy-start(f32[1,3352,8]{1,2,0:T(8,128)} %param.32) | copy-start | bytes 321796
  7.3 46.8 %all-gather.3.cloned.1.call-start = ((), (), s32[]{:S(2)}) async-start(), calls=%async_computation.2 | async-start | bytes 6635520 | tf_op jit(solution)/shard_map/all_gather | solution.py:146
  10.4 382.1 %all-gather.5.cloned.1.call-start = ((), (), s32[]{:S(2)}) async-start(), calls=%async_computation.3 | async-start | bytes 2949120 | tf_op jit(solution)/shard_map/all_gather | solution.py:147
  12.6 1104.8 %reduce-scatter.5.cloned.1.call-start = ((), (), s32[]{:S(2)}) async-start(), calls=%async_computation.5 | async-start | bytes 5898240 | tf_op jit(solution)/shard_map/reduce_scatter | solution.py:195
  12.8 81.5 %copy-start.58 = (f32[24]{0:T(128)}, f32[24]{0:T(128)S(1)}, u32[]{:S(2)}) copy-start(f32[24]{0:T(128)S(1)} %get-tuple-element.1044) | copy-start | bytes 292
  12.8 81.5 %copy-start.60 = (f32[24]{0:T(128)}, f32[24]{0:T(128)S(1)}, u32[]{:S(2)}) copy-start(f32[24]{0:T(128)S(1)} %get-tuple-element.1045) | copy-start | bytes 292
  13.9 387.3 %copy-start.23 = (f32[1536]{0:T(1024)}, f32[1536]{0:T(1024)S(1)}, u32[]{:S(2)}) copy-start(f32[1536]{0:T(1024)S(1)} %mul.2216) | copy-start | bytes 18436
  14.0 61.4 %copy-start.27 = (f32[1792]{0:T(1024)}, f32[1792]{0:T(1024)S(1)}, u32[]{:S(2)}) copy-start(f32[1792]{0:T(1024)S(1)} %get-tuple-element.791) | copy-start | bytes 21508
  14.0 61.4 %copy-start.29 = (f32[1792]{0:T(1024)}, f32[1792]{0:T(1024)S(1)}, u32[]{:S(2)}) copy-start(f32[1792]{0:T(1024)S(1)} %get-tuple-element.789) | copy-start | bytes 21508
  14.0 61.4 %copy-start.31 = (f32[1792]{0:T(1024)}, f32[1792]{0:T(1024)S(1)}, u32[]{:S(2)}) copy-start(f32[1792]{0:T(1024)S(1)} %get-tuple-element.788) | copy-start | bytes 21508
  14.0 61.4 %copy-start.33 = (f32[1792]{0:T(1024)}, f32[1792]{0:T(1024)S(1)}, u32[]{:S(2)}) copy-start(f32[1792]{0:T(1024)S(1)} %get-tuple-element.790) | copy-start | bytes 21508
  14.1 61.2 %copy-start.37 = (f32[1,1024]{1,0:T(1,128)}, f32[1,1024]{1,0:T(1,128)S(1)}, u32[]{:S(2)}) copy-start(f32[1,1024]{1,0:T(1,128)S(1)} %get-tuple-element.1040) | copy-start | bytes 12292
  14.1 61.2 %copy-start.39 = (f32[1,1024]{1,0:T(1,128)}, f32[1,1024]{1,0:T(1,128)S(1)}, u32[]{:S(2)}) copy-start(f32[1,1024]{1,0:T(1,128)S(1)} %get-tuple-element.1041) | copy-start | bytes 12292
  14.2 61.2 %copy-start.43 = (f32[1,1024]{1,0:T(1,128)}, f32[1,1024]{1,0:T(1,128)S(1)}, u32[]{:S(2)}) copy-start(f32[1,1024]{1,0:T(1,128)S(1)} %get-tuple-element.1042) | copy-start | bytes 12292
  401.1 819.6 %reduce-scatter.3.cloned.1.call-start = ((), (), s32[]{:S(2)}) async-start(), calls=%async_computation.4 | async-start | bytes 13271040 | tf_op jit(solution)/shard_map/reduce_scatter | solution.py:194
  1043.6 345.6 %all-reduce.29.cloned.1.call-start = ((), (), s32[]{:S(2)}) async-start(), calls=%async_computation.6 | async-start | bytes 221184 | tf_op jit(solution)/shard_map/psum | solution.py:210
  1045.8 58.8 %copy-start.46 = (f32[1536]{0:T(1024)S(1)}, f32[1536]{0:T(1024)}, u32[]{:S(2)}) copy-start(f32[1536]{0:T(1024)} %param.40) | copy-start | bytes 18436
  1045.8 58.8 %copy-start.55 = (f32[1536]{0:T(1024)S(1)}, f32[1536]{0:T(1024)}, u32[]{:S(2)}) copy-start(f32[1536]{0:T(1024)} %param.41) | copy-start | bytes 18436
  1045.9 59.4 %copy-start.22 = (f32[5,1792]{1,0:T(8,128)S(1)}, f32[5,1792]{1,0:T(8,128)}, u32[]{:S(2)}) copy-start(f32[5,1792]{1,0:T(8,128)} %param.34) | copy-start | bytes 107524
  1045.9 59.4 %copy-start.35 = (f32[5,1792]{1,0:T(8,128)S(1)}, f32[5,1792]{1,0:T(8,128)}, u32[]{:S(2)}) copy-start(f32[5,1792]{1,0:T(8,128)} %param.35) | copy-start | bytes 107524
  1045.9 60.0 %copy-start.15 = (bf16[1,1024,768]{2,1,0:T(8,128)(2,1)S(1)}, bf16[1,1024,768]{2,1,0:T(8,128)(2,1)}, u32[]{:S(2)}) copy-start(bf16[1,1024,768]{2,1,0:T(8,128)(2,1)} %param.25) | copy-start | bytes 4718596
  1117.4 103.4 %copy-start.8 = (f32[1,192,3352]{2,1,0:T(8,128)S(1)}, f32[1,192,3352]{2,1,0:T(8,128)}, u32[]{:S(2)}) copy-start(f32[1,192,3352]{2,1,0:T(8,128)} %param.28) | copy-start | bytes 7723012
  1218.4 103.5 %copy-start.25 = (f32[384,8]{0,1:T(8,128)}, f32[384,8]{0,1:T(8,128)S(1)}, u32[]{:S(2)}) copy-start(f32[384,8]{0,1:T(8,128)S(1)} %stack.5) | copy-start | bytes 36868
  1317.8 72.9 %copy-start.26 = (f32[192,8]{0,1:T(8,128)}, f32[192,8]{0,1:T(8,128)S(1)}, u32[]{:S(2)}) copy-start(f32[192,8]{0,1:T(8,128)S(1)} %stack.4) | copy-start | bytes 18436
  (72 other events, 918.0 us)
Sparse Core Ops, SparseCore 0:
  10.5 43.4 all-gather.2
  56.2 24.0 all-gather.4
  401.3 47.9 reduce-scatter.4
  1043.7 85.9 reduce-scatter.2
  1322.0 67.0 all-reduce.28
where the time goes:
time: 1430 us; the launch traced here: 1410 us
  local copies, waits for them, and re-layouts  541 us (38%)
  other arithmetic  333 us (23%)
  matrix products  282 us (20%)
  blocking collectives  112 us (8%)
  waiting for transfers between devices  101 us (7%)
  between operations  25.8 us (2%)
    dynamic_update_slice x32, local copies, waits for them, and re-layouts, spanned_scan(): ended, outputs = lax.scan(jax.checkpoint(span_step), start, pieces)  352 us
    dot_general x12, matrix products, span_step(): local_out = jnp.einsum('hij,jhp->ihp', mixing, heads_vals, precision=HIGH)  107 us
    psum x2, blocking collectives, on_device(): left_in, left_out = lax.psum((left_in, left_out), 'rep')  70.4 us
    psum x1, waiting for transfers between devices, on_device(): right_in, right_out = lax.psum((right_in, right_out), 'rep')  61.1 us
    reduce_sum x20, other arithmetic, orthogonal(): vector = vector - jnp.sum(done * vector) * done  58.9 us
    psum x1, blocking collectives, on_device(): lax.psum((d_conv, d_heads, d_norm_gain, d_gate_gain), ('grp', 'rep'))  41.2 us
    all_gather x1, waiting for transfers between devices, on_device(): lax.all_gather(in_proj_master.astype(jnp.bfloat16), 'grp', axis=0, tiled=...  39.9 us
    dot_general x16, matrix products, span_step(): carried = jnp.einsum('in,hpn->ihp', out_c, state, precision=HIGH)  39.5 us
  transfers between devices with their start and end apart: 5, of which 2 were waited for; matrix products, arithmetic and copies ran while one was open for 76% of the time, Pallas kernels for 0%

commit v1 on v0

--- a/solution.py
+++ b/solution.py
@@ -143,7 +143,12 @@
 ):
     replicas = lax.axis_size("rep")
     w_in, w_out = (
-        lax.all_gather(in_proj_master.astype(jnp.bfloat16), "grp", axis=0, tiled=True),
+        jnp.concatenate(
+            lax.all_to_all(
+                jnp.stack([in_proj_master.astype(jnp.bfloat16)] * lax.axis_size("grp")), "grp", 0, 0
+            ),
+            axis=0,
+        ),
         lax.all_gather(out_proj_master.astype(jnp.bfloat16), "grp", axis=0, tiled=True),
     )
     seq_count, seq_len, width = tokens.shape

time: 1430 us -> 1470 us (1.028)
  waiting for transfers between devices: 101 us -> 131 us
    all_to_all x0 -> x1, waiting for transfers between devices: none -> 69.7 us  [on_device(): lax.all_to_all(jnp.stack([in_proj_master.astype(jnp.bfloat16)] * lax.axis...]
    all_gather x1 -> x0, waiting for transfers between devices: 39.9 us -> none  [on_device(): lax.all_gather(in_proj_master.astype(jnp.bfloat16), 'grp', axis=0, tiled=...]
    another operation x90 -> x91, local copies, waits for them, and re-layouts: 32.3 us -> 35 us
  transfers between devices with their start and end apart: 5 -> 5, of which waited for: 2 -> 2; matrix products, arithmetic and copies ran while one was open for 76% -> 74% of each run, Pallas kernels for 0% -> 0%
where the time goes in v1:
time: 1470 us; the launch traced here: 1440 us
  local copies, waits for them, and re-layouts  543 us (37%)
  other arithmetic  331 us (23%)
  matrix products  281 us (19%)
  waiting for transfers between devices  131 us (9%)
  blocking collectives  114 us (8%)
  between operations  25.8 us (2%)
    dynamic_update_slice x32, local copies, waits for them, and re-layouts, spanned_scan(): ended, outputs = lax.scan(jax.checkpoint(span_step), start, pieces)  352 us
    dot_general x12, matrix products, span_step(): local_out = jnp.einsum('hij,jhp->ihp', mixing, heads_vals, precision=HIGH)  107 us
    psum x2, blocking collectives, on_device(): left_in, left_out = lax.psum((left_in, left_out), 'rep')  70.4 us
    all_to_all x1, waiting for transfers between devices, on_device(): lax.all_to_all(jnp.stack([in_proj_master.astype(jnp.bfloat16)] * lax.axis...  69.7 us
    psum x1, waiting for transfers between devices, on_device(): right_in, right_out = lax.psum((right_in, right_out), 'rep')  61.1 us
    reduce_sum x20, other arithmetic, orthogonal(): vector = vector - jnp.sum(done * vector) * done  58.9 us
    psum x1, blocking collectives, on_device(): lax.psum((d_conv, d_heads, d_norm_gain, d_gate_gain), ('grp', 'rep'))  43.9 us
    dot_general x16, matrix products, span_step(): carried = jnp.einsum('in,hpn->ihp', out_c, state, precision=HIGH)  39.5 us
  transfers between devices with their start and end apart: 5, of which 2 were waited for; matrix products, arithmetic and copies ran while one was open for 74% of the time, Pallas kernels for 0%

profile of v1, /device:TPU:0, one launch (start us, length us, event | category | flops | bytes accessed | tf_op | source)
XLA Modules:
  0.0 1444.7 jit_solution(7421602638242624870)
XLA Ops:
  20.8 69.7 %all-to-all-done = bf16[4,192,3352]{2,1,0:T(8,128)(2,1)} async-done(((bf16[4,192,3352]{2,1,0:T(8,128)(2,1)}), bf16[4,192,3352]{2,1,0:T(8,128)(2,1)}, u32[]{:S(2)}, u32[]{:S(2)}) %all-to-all-start) | async-done | bytes 5148704 | tf_op jit(solution)/shard_map/all_to_all | solution.py:147
  111.9 15.0 %multiply_convert_fusion = (bf16[1,1024,1792]{1,2,0:T(8,128)(2,1)S(1)}, f32[1,1024,1792]{1,2,0:T(8,128)}) fusion(f32[1024]{0:T(1024)S(1)} %bitcast.694, f32[1,1021,1792]{1,2,0:T(8,128)} %slice.251, f32[1792]{0:T(1024)S(1)} %get-tuple-element.791, f32[1024]{0:T(1024)S(1)} %bitcast.692, f32[1,1022,1792]{1,2,0:T(8,128)} %slice.250, ...), kind=kLoop, calls=%fused_computation.159 | loop fusion | flops 29360128 | bytes 40375296 | tf_op jit(solution)/shard_map/convert_element_type | solution.py:171
  145.2 254.0 %while.46 = (s32[]{:T(128)}, f32[1,24,64,128]{3,2,1,0:T(8,128)S(1)}, s32[1]{0:T(128)}, f32[4,1,256,1536]{2,0,3,1:T(4,128)}, f32[4,1,24,64,128]{4,3,2,1,0:T(8,128...) while((s32[]{:T(128)}, ...), condition=%wide.region_4.5_spmd.clone, body=%wide.region_1.4_spmd.clone.sunk | while | flops 2527624192 | bytes 27957864 | solution.py:81
  173.9 34.1 %dynamic_update_slice.88 = f32[4,1,256,1536]{2,0,3,1:T(4,128)} dynamic-update-slice(f32[4,1,256,1536]{2,0,3,1:T(4,128)} %get-tuple-element.1300, f32[1,1,256,1536]{2,0,3,1:T(1,128)S(1)} %copy.412, s32[]{:T(128)S(6)} %copy.447, s32[]{:T(128)} %constant.161.clone.1..sunk, s32[]{:T(128)} %constant.161.clone.1..sunk, s32[]{:T(128)} %constant.161.clone.1..sunk) | dynamic-update-slice | bytes 3145732 | tf_op jit(solution)/shard_map/jvp(vmap())/while/body/jit(dynamic_update_index_in_dim)/dynamic_update_slice | solution.py:81
  237.4 34.1 %dynamic_update_slice.88 = f32[4,1,256,1536]{2,0,3,1:T(4,128)} dynamic-update-slice(f32[4,1,256,1536]{2,0,3,1:T(4,128)} %get-tuple-element.1300, f32[1,1,256,1536]{2,0,3,1:T(1,128)S(1)} %copy.412, s32[]{:T(128)S(6)} %copy.447, s32[]{:T(128)} %constant.161.clone.1..sunk, s32[]{:T(128)} %constant.161.clone.1..sunk, s32[]{:T(128)} %constant.161.clone.1..sunk) | dynamic-update-slice | bytes 3145732 | tf_op jit(solution)/shard_map/jvp(vmap())/while/body/jit(dynamic_update_index_in_dim)/dynamic_update_slice | solution.py:81
  300.9 34.1 %dynamic_update_slice.88 = f32[4,1,256,1536]{2,0,3,1:T(4,128)} dynamic-update-slice(f32[4,1,256,1536]{2,0,3,1:T(4,128)} %get-tuple-element.1300, f32[1,1,256,1536]{2,0,3,1:T(1,128)S(1)} %copy.412, s32[]{:T(128)S(6)} %copy.447, s32[]{:T(128)} %constant.161.clone.1..sunk, s32[]{:T(128)} %constant.161.clone.1..sunk, s32[]{:T(128)} %constant.161.clone.1..sunk) | dynamic-update-slice | bytes 3145732 | tf_op jit(solution)/shard_map/jvp(vmap())/while/body/jit(dynamic_update_index_in_dim)/dynamic_update_slice | solution.py:81
  364.5 34.1 %dynamic_update_slice.88 = f32[4,1,256,1536]{2,0,3,1:T(4,128)} dynamic-update-slice(f32[4,1,256,1536]{2,0,3,1:T(4,128)} %get-tuple-element.1300, f32[1,1,256,1536]{2,0,3,1:T(1,128)S(1)} %copy.412, s32[]{:T(128)S(6)} %copy.447, s32[]{:T(128)} %constant.161.clone.1..sunk, s32[]{:T(128)} %constant.161.clone.1..sunk, s32[]{:T(128)} %constant.161.clone.1..sunk) | dynamic-update-slice | bytes 3145732 | tf_op jit(solution)/shard_map/jvp(vmap())/while/body/jit(dynamic_update_index_in_dim)/dynamic_update_slice | solution.py:81
  437.6 18.9 %multiply_reduce_fusion.8 = (f32[1536]{0:T(1024)}, f32[1,1024,1536]{1,2,0:T(8,128)}, f32[1,1024,1536]{1,2,0:T(8,128)}) fusion(f32[1,1024,1792]{1,2,0:T(8,128)} %convert_element_type.87, f32[1,1024,3352]{1,2,0:T(8,128)} %copy-done.1, f32[1,1024,1536]{1,2,0:T(8,128)} %copy-done.7, f32[1024]{0:T(1024)S(1)} %multiply_multiply_fusion.1, f32[1024]{0:T(1024)S(1)} %fusion.124, ...), kind=kLoop, calls=%fused_computation.170 | loop fusion | flops 33028608 | bytes 44066816 | tf_op jit(solution)/shard_map/transpose(jvp(vmap()))/reduce_sum | solution.py:92
  471.0 512.2 %while.47 = (s32[]{:T(128)}, f32[1,24,64,128]{3,2,1,0:T(8,128)S(1)}, f32[4,1,256,1536]{2,0,3,1:T(4,128)}, f32[4,1,24,256]{2,3,1,0:T(8,128)}, f32[4,1,24,256]{3,0...) while((s32[]{:T(128)}, ...), condition=%wide.region_20.21_spmd.clone, body=%wide.region_7.20_spmd.clone.sunk | while | flops 5775293440 | bytes 58667620 | solution.py:81
  565.0 34.1 %dynamic_update_slice.92 = f32[4,1,256,1536]{2,0,3,1:T(4,128)} dynamic-update-slice(f32[4,1,256,1536]{2,0,3,1:T(4,128)} %get-tuple-element.1349, f32[1,1,256,1536]{2,0,3,1:T(1,128)S(1)} %copy.427, s32[]{:T(128)S(6)} %sub.1200, s32[]{:T(128)} %constant.161.clone.1..sunk.1, s32[]{:T(128)} %constant.161.clone.1..sunk.1, s32[]{:T(128)} %constant.161.clone.1..sunk.1) | dynamic-update-slice | bytes 3145732 | tf_op jit(solution)/shard_map/transpose(jvp(vmap()))/while/body/jit(dynamic_update_index_in_dim)/dynamic_update_slice | solution.py:81
  693.0 34.1 %dynamic_update_slice.92 = f32[4,1,256,1536]{2,0,3,1:T(4,128)} dynamic-update-slice(f32[4,1,256,1536]{2,0,3,1:T(4,128)} %get-tuple-element.1349, f32[1,1,256,1536]{2,0,3,1:T(1,128)S(1)} %copy.427, s32[]{:T(128)S(6)} %sub.1200, s32[]{:T(128)} %constant.161.clone.1..sunk.1, s32[]{:T(128)} %constant.161.clone.1..sunk.1, s32[]{:T(128)} %constant.161.clone.1..sunk.1) | dynamic-update-slice | bytes 3145732 | tf_op jit(solution)/shard_map/transpose(jvp(vmap()))/while/body/jit(dynamic_update_index_in_dim)/dynamic_update_slice | solution.py:81
  762.5 12.0 fusion.249
  820.9 34.1 %dynamic_update_slice.92 = f32[4,1,256,1536]{2,0,3,1:T(4,128)} dynamic-update-slice(f32[4,1,256,1536]{2,0,3,1:T(4,128)} %get-tuple-element.1349, f32[1,1,256,1536]{2,0,3,1:T(1,128)S(1)} %copy.427, s32[]{:T(128)S(6)} %sub.1200, s32[]{:T(128)} %constant.161.clone.1..sunk.1, s32[]{:T(128)} %constant.161.clone.1..sunk.1, s32[]{:T(128)} %constant.161.clone.1..sunk.1) | dynamic-update-slice | bytes 3145732 | tf_op jit(solution)/shard_map/transpose(jvp(vmap()))/while/body/jit(dynamic_update_index_in_dim)/dynamic_update_slice | solution.py:81
  948.8 34.1 %dynamic_update_slice.92 = f32[4,1,256,1536]{2,0,3,1:T(4,128)} dynamic-update-slice(f32[4,1,256,1536]{2,0,3,1:T(4,128)} %get-tuple-element.1349, f32[1,1,256,1536]{2,0,3,1:T(1,128)S(1)} %copy.427, s32[]{:T(128)S(6)} %sub.1200, s32[]{:T(128)} %constant.161.clone.1..sunk.1, s32[]{:T(128)} %constant.161.clone.1..sunk.1, s32[]{:T(128)} %constant.161.clone.1..sunk.1) | dynamic-update-slice | bytes 3145732 | tf_op jit(solution)/shard_map/transpose(jvp(vmap()))/while/body/jit(dynamic_update_index_in_dim)/dynamic_update_slice | solution.py:81
  1005.5 13.0 multiply_reduce_fusion.7
  1049.4 14.6 %multiply_reduce_fusion.4 = (f32[1792]{0:T(1024)S(1)}, f32[1792]{0:T(1024)S(1)}, f32[1,1024,1792]{1,2,0:T(8,128)}) fusion(f32[1,1024,1792]{1,2,0:T(8,128)S(1)} %bitcast.642, f32[1,1024,3352]{1,2,0:T(8,128)} %copy-done.1, f32[1792]{0:T(1024)S(1)} %copy-done.34, f32[1,1023,1792]{1,2,0:T(8,128)} %slice_multiply_fusion, ...), kind=kLoop, calls=%fused_computation.154 | loop fusion | flops 12841472 | bytes 44018688 | tf_op jit(solution)/shard_map/transpose(jvp(vmap()))/reduce_sum | solution.py:32
  1064.1 15.2 %fusion.107 = f32[768,3352]{1,0:T(8,128)} fusion(bf16[1,1024,768]{2,1,0:T(8,128)(2,1)S(1)} %copy-done.13, f32[768]{0:T(1024)S(1)} %copy-done.50, f32[1024]{0:T(1024)S(1)} %copy-done.52, f32[1,1024,1536]{1,2,0:T(8,128)} %get-tuple-element.1023, f32[1,1024,1792]{1,2,0:T(8,128)} %get-tuple-element.1024, f32[1,1024,24]{1,2,0:T(8,128)S(1)} %get-tuple-element.931), kind=kOutput, calls=%fused_computation.210 | convolution fusion | flops 5285683200 | bytes 25607168 | tf_op jit(solution)/shard_map/dot_general | solution.py:109
  1081.6 13.0 fusion.94
  1094.6 43.9 %all-reduce.25 = (f32[5,1792]{1,0:T(8,128)S(1)}, f32[3,24]{1,0:T(4,128)S(1)}, f32[768]{0:T(1024)S(1)}, f32[1536]{0:T(1024)S(1)}) all-reduce(f32[5,1792]{1,0:T(8,128)S(1)} %pad_add_fusion, f32[3,24]{1,0:T(4,128)} %add_add_fusion.2, f32[768]{0:T(1024)} %get-tuple-element.785, ...), channel_id=1, replica_groups=mesh['grp'=4,'rep'=8] {'grp','rep'}, use_global_device_ids=true, to_apply=%region_105.106 | all-reduce | flops 11336 | bytes 90688 | tf_op jit(solution)/shard_map/psum | solution.py:207
  1157.7 37.0 %psum.57 = f32[384,8]{0,1:T(8,128)S(1)} all-reduce(f32[384,8]{0,1:T(8,128)S(1)} %fusion.118), channel_id=1, replica_groups=mesh['grp'=4,'rep'=8] {'rep'}, use_global_device_ids=true, to_apply=%region_61.62 | all-reduce | flops 3072 | bytes 24576 | tf_op jit(solution)/shard_map/psum | solution.py:210
  1238.0 17.7 %subtract_multiply_fusion.2 = (f32[384,1]{0,1:T(1,128)S(1)}, f32[384,1]{0,1:T(1,128)S(1)}, f32[384,1]{0,1:T(1,128)S(1)}, f32[384,1]{0,1:T(1,128)S(1)}, f32[384,1...) fusion(f32[384,1]{0,1:T(1,128)S(1)} %get-tuple-element.1004, f32[384,8]{0,1:T(8,128)S(1)} %psum.57, ...), kind=kLoop, calls=%fused_computation.318 | loop fusion | flops 24192 | bytes 23180 | tf_op jit(solution)/shard_map/mul | solution.py:103
  1262.3 33.4 %all-reduce.26 = (f32[192,8]{0,1:T(8,128)S(1)}, f32[768,8]{0,1:T(8,128)S(1)}) all-reduce(f32[192,8]{0,1:T(8,128)S(1)} %fusion.110, f32[768,8]{0,1:T(8,128)S(1)} %fusion.128), channel_id=1, replica_groups=mesh['grp'=4,'rep'=8] {'rep'}, use_global_device_ids=true, to_apply=%region_24.25 | all-reduce | flops 7680 | bytes 61440 | tf_op jit(solution)/shard_map/psum | solution.py:210
  1337.6 17.6 %subtract_multiply_fusion.9 = (f32[192,1]{0,1:T(1,128)S(1)}, f32[192,1]{0,1:T(1,128)S(1)}, f32[192,1]{0,1:T(1,128)S(1)}, f32[192,1]{0,1:T(1,128)S(1)}, f32[192,1...) fusion(f32[192,1]{0,1:T(1,128)S(1)} %get-tuple-element.1033, f32[]{:T(128)S(6)} %rsqrt.79, ...), kind=kLoop, calls=%fused_computation.331 | loop fusion | flops 12096 | bytes 11660 | tf_op jit(solution)/shard_map/mul | solution.py:103
  1365.5 61.1 %all-reduce.29.cloned.1.call-done = f32[3352,8]{0,1:T(8,128)} async-done(((f32[3352,8]{0,1:T(8,128)}), f32[3352,8]{0,1:T(8,128)}) %all-reduce.29.cloned.1.call-update) | async-done | bytes 107280 | tf_op jit(solution)/shard_map/psum | solution.py:215
  (693 shorter events, 751.2 us)
Async XLA Ops:
  7.2 1251.0 %copy-start = (f32[1,3352,8]{1,2,0:T(8,128)S(1)}, f32[1,3352,8]{1,2,0:T(8,128)}, u32[]{:S(2)}) copy-start(f32[1,3352,8]{1,2,0:T(8,128)} %param.32) | copy-start | bytes 321796
  11.8 78.7 %copy-start.49 = (f32[768]{0:T(1024)S(1)}, f32[768]{0:T(1024)}, u32[]{:S(2)}) copy-start(f32[768]{0:T(1024)} %param.38) | copy-start | bytes 9220
  11.8 78.7 %all-to-all-start = ((bf16[4,192,3352]{2,1,0:T(8,128)(2,1)}), bf16[4,192,3352]{2,1,0:T(8,128)(2,1)}, u32[]{:S(2)}, u32[]{:S(2)}) async-start(bf16[4,192,3352]{2,1,0:T(8,128)(2,1)} %stack.6), calls=%async_computation | async-start | bytes 10616832 | tf_op jit(solution)/shard_map/all_to_all | solution.py:147
  17.1 411.9 %all-gather.2.cloned.1.call-start = ((), (), s32[]{:S(2)}) async-start(), calls=%async_computation.3 | async-start | bytes 2949120 | tf_op jit(solution)/shard_map/all_gather | solution.py:152
  19.3 1135.5 %reduce-scatter.5.cloned.1.call-start = ((), (), s32[]{:S(2)}) async-start(), calls=%async_computation.5 | async-start | bytes 5898240 | tf_op jit(solution)/shard_map/reduce_scatter | solution.py:200
  19.4 111.4 %copy-start.58 = (f32[24]{0:T(128)}, f32[24]{0:T(128)S(1)}, u32[]{:S(2)}) copy-start(f32[24]{0:T(128)S(1)} %get-tuple-element.1044) | copy-start | bytes 292
  19.4 111.4 %copy-start.60 = (f32[24]{0:T(128)}, f32[24]{0:T(128)S(1)}, u32[]{:S(2)}) copy-start(f32[24]{0:T(128)S(1)} %get-tuple-element.1045) | copy-start | bytes 292
  19.6 418.0 %copy-start.23 = (f32[1536]{0:T(1024)}, f32[1536]{0:T(1024)S(1)}, u32[]{:S(2)}) copy-start(f32[1536]{0:T(1024)S(1)} %mul.2216) | copy-start | bytes 18436
  19.7 92.2 %copy-start.27 = (f32[1792]{0:T(1024)}, f32[1792]{0:T(1024)S(1)}, u32[]{:S(2)}) copy-start(f32[1792]{0:T(1024)S(1)} %get-tuple-element.791) | copy-start | bytes 21508
  19.7 92.2 %copy-start.29 = (f32[1792]{0:T(1024)}, f32[1792]{0:T(1024)S(1)}, u32[]{:S(2)}) copy-start(f32[1792]{0:T(1024)S(1)} %get-tuple-element.789) | copy-start | bytes 21508
  19.7 92.2 %copy-start.31 = (f32[1792]{0:T(1024)}, f32[1792]{0:T(1024)S(1)}, u32[]{:S(2)}) copy-start(f32[1792]{0:T(1024)S(1)} %get-tuple-element.788) | copy-start | bytes 21508
  19.7 92.2 %copy-start.33 = (f32[1792]{0:T(1024)}, f32[1792]{0:T(1024)S(1)}, u32[]{:S(2)}) copy-start(f32[1792]{0:T(1024)S(1)} %get-tuple-element.790) | copy-start | bytes 21508
  20.1 78.7 %copy-start.51 = (f32[1024]{0:T(1024)}, f32[1024]{0:T(1024)S(1)}, u32[]{:S(2)}) copy-start(f32[1024]{0:T(1024)S(1)} %fusion.123) | copy-start | bytes 12292
  20.8 91.1 %copy-start.37 = (f32[1,1024]{1,0:T(1,128)}, f32[1,1024]{1,0:T(1,128)S(1)}, u32[]{:S(2)}) copy-start(f32[1,1024]{1,0:T(1,128)S(1)} %get-tuple-element.1040) | copy-start | bytes 12292
  20.8 91.1 %copy-start.39 = (f32[1,1024]{1,0:T(1,128)}, f32[1,1024]{1,0:T(1,128)S(1)}, u32[]{:S(2)}) copy-start(f32[1,1024]{1,0:T(1,128)S(1)} %get-tuple-element.1041) | copy-start | bytes 12292
  20.8 91.1 %copy-start.43 = (f32[1,1024]{1,0:T(1,128)}, f32[1,1024]{1,0:T(1,128)S(1)}, u32[]{:S(2)}) copy-start(f32[1,1024]{1,0:T(1,128)S(1)} %get-tuple-element.1042) | copy-start | bytes 12292
  437.5 820.6 %reduce-scatter.3.cloned.1.call-start = ((), (), s32[]{:S(2)}) async-start(), calls=%async_computation.4 | async-start | bytes 13271040 | tf_op jit(solution)/shard_map/reduce_scatter | solution.py:199
  1079.3 347.2 %all-reduce.29.cloned.1.call-start = ((), (), s32[]{:S(2)}) async-start(), calls=%async_computation.6 | async-start | bytes 221184 | tf_op jit(solution)/shard_map/psum | solution.py:215
  1081.6 61.1 %copy-start.22 = (f32[5,1792]{1,0:T(8,128)S(1)}, f32[5,1792]{1,0:T(8,128)}, u32[]{:S(2)}) copy-start(f32[5,1792]{1,0:T(8,128)} %param.34) | copy-start | bytes 107524
  1081.6 61.1 %copy-start.35 = (f32[5,1792]{1,0:T(8,128)S(1)}, f32[5,1792]{1,0:T(8,128)}, u32[]{:S(2)}) copy-start(f32[5,1792]{1,0:T(8,128)} %param.35) | copy-start | bytes 107524
  1081.6 61.7 %copy-start.15 = (bf16[1,1024,768]{2,1,0:T(8,128)(2,1)S(1)}, bf16[1,1024,768]{2,1,0:T(8,128)(2,1)}, u32[]{:S(2)}) copy-start(bf16[1,1024,768]{2,1,0:T(8,128)(2,1)} %param.25) | copy-start | bytes 4718596
  1154.8 103.4 %copy-start.8 = (f32[1,192,3352]{2,1,0:T(8,128)S(1)}, f32[1,192,3352]{2,1,0:T(8,128)}, u32[]{:S(2)}) copy-start(f32[1,192,3352]{2,1,0:T(8,128)} %param.28) | copy-start | bytes 7723012
  1255.8 103.5 %copy-start.25 = (f32[384,8]{0,1:T(8,128)}, f32[384,8]{0,1:T(8,128)S(1)}, u32[]{:S(2)}) copy-start(f32[384,8]{0,1:T(8,128)S(1)} %stack.8) | copy-start | bytes 36868
  1355.2 72.9 %copy-start.26 = (f32[192,8]{0,1:T(8,128)}, f32[192,8]{0,1:T(8,128)S(1)}, u32[]{:S(2)}) copy-start(f32[192,8]{0,1:T(8,128)S(1)} %stack.7) | copy-start | bytes 18436
  (72 other events, 955.5 us)
Sparse Core Ops, SparseCore 0:
  20.0 39.9 all-gather.1
  437.7 49.0 reduce-scatter.4
  1079.4 87.7 reduce-scatter.2
  1359.4 67.0 all-reduce.28
